TPU v7x, 256 devices: a whole 4x4x8 slice. The times are simulated.
256 devices in a mesh: section: 16 (over y_hi, x, core), tensor: 16 (over y_lo, z).
Axes of the slice: x: 4, y: 4 (y_hi: 2, y_lo: 2; y = y_hi * 2 + y_lo), z: 8, core: 2. Of those that a mesh axis runs over, the one named last changes fastest.
Arguments:
- state: bfloat16 [16, 256, 6144], P('section', None, 'tensor'), may hold values from -6 to 6
- ln_gain: float32 [16, 6144], P('section'), may hold values from 0.1 to 1.9
- w_qkv: bfloat16 [16, 6144, 3, 4096], P('section', None, None, 'tensor'), may hold values from -0.078125 to 0.078125
- qk_gain: float32 [16, 2, 128], P('section'), may hold values from 0.5 to 1.5
- w_out: bfloat16 [16, 4096, 6144], P('section', 'tensor'), may hold values from -1 to 1
Outputs:
- advanced: bfloat16 [16, 256, 6144], P('section', None, 'tensor')
All inputs are finite; a program needn't handle non-finite values.
Results may differ from a plain program's by a relative error of at most 0.03.
Values may be sent and summed in bfloat16 or wider, within the bound.
No kernel may reach another device: no remote copies, remote signals or barrier semaphores. Data moves between devices by JAX's collectives and lax.ppermute only.
A program may use at most 128 MiB of HBM per device.

v0:
```python
import jax
import jax.numpy as jnp
from jax import lax
from jax.sharding import PartitionSpec as P

HD = 128
STEPS = 2


def passed_along(shard, axis, by):
    peers = lax.axis_size(axis)
    return lax.ppermute(shard, axis, [(i, (i + by) % peers) for i in range(peers)])


def layer_norm(values, gain):
    mean = jnp.mean(values, axis=-1, keepdims=True)
    squares = jnp.mean(values * values, axis=-1, keepdims=True)
    spread = squares - mean * mean
    return (values - mean) * lax.rsqrt(spread + 1e-06) * gain


def on_device(state, ln_gain, w_qkv, qk_gain, w_out):
    current = state[0]
    patches = current.shape[0]
    full_width = w_qkv.shape[1]
    head_cols = w_qkv.shape[3]
    local_heads = head_cols // HD
    qkv_flat = w_qkv[0].reshape(full_width, 3 * head_cols)
    out_local = w_out[0]
    gain_row = ln_gain[0]
    norm_gains = qk_gain[0]
    for step_index in range(STEPS):
        gathered = lax.all_gather(current, "tensor", axis=1, tiled=True)
        normed = layer_norm(gathered.astype(jnp.float32), gain_row).astype(jnp.bfloat16)
        projected = jnp.dot(normed, qkv_flat, preferred_element_type=jnp.float32)
        projected = projected.reshape(patches, 3, local_heads, HD)
        query = layer_norm(projected[:, 0], norm_gains[0]).astype(jnp.bfloat16)
        keys_all = layer_norm(projected[:, 1], norm_gains[1]).astype(jnp.bfloat16)
        value = projected[:, 2].astype(jnp.bfloat16)
        scores = jnp.einsum(
            "phe,qhe->hpq", query, keys_all, preferred_element_type=jnp.float32
        ) / jnp.sqrt(jnp.float32(HD))
        expo = jnp.exp(scores)
        attend = (expo / jnp.sum(expo, axis=-1, keepdims=True)).astype(jnp.bfloat16)
        mixed_rows = jnp.einsum("hpq,qhe->phe", attend, value, preferred_element_type=jnp.float32)
        mixed_rows = mixed_rows.astype(jnp.bfloat16).reshape(patches, head_cols)
        branch = lax.psum_scatter(
            lax.dot_general(
                out_local, mixed_rows, (((0,), (1,)), ((), ())), preferred_element_type=jnp.float32
            ).astype(jnp.bfloat16),
            "tensor",
            scatter_dimension=0,
            tiled=True,
        ).astype(jnp.float32)
        renewed = (current.astype(jnp.float32) + branch.T).astype(jnp.bfloat16)
        current = passed_along(renewed, "section", 1)
    return current[None]


def solution(mesh):
    placed = (
        P("section", None, "tensor"),
        P("section", None),
        P("section", None, None, "tensor"),
        P("section", None, None),
        P("section", "tensor", None),
    )
    return jax.shard_map(
        on_device,
        mesh=mesh,
        in_specs=placed,
        out_specs=P("section", None, "tensor"),
        check_vma=False,
    )
```

profile of v0, /device:TPU:16, one launch (start us, length us, event | category | flops | bytes accessed | tf_op | source)
XLA Modules:
  0.0 375.9 jit_solution(2082185066389066385)
XLA Ops:
  7.3 12.9 %copy.19 = bf16[1,6144,3,256]{1,3,2,0:T(8,128)(2,1)} copy(bf16[1,6144,3,256]{3,1,2,0:T(8,128)(2,1)} %param.7) | data formatting | bytes 18874368 | tf_op args[2]
  20.2 65.4 %all-gather.6.cloned.1.call-done = bf16[1,256,6144]{2,1,0:T(8,128)(2,1)} async-done(((bf16[1,256,384]{2,1,0:T(8,128)(2,1)}), bf16[1,256,6144]{2,1,0:T(8,128)(2,1)}) %all-gather.6.cloned.1.call-update) | async-done | bytes 3145744 | tf_op jit(solution)/shard_map/all_gather | solution.py:33
  85.6 2.5 convert_reduce_fusion.1
  88.2 2.6 fusion.4
  90.8 6.0 %fusion.16 = f32[256,3,2,128]{0,3,2,1:T(8,128)S(1)} fusion(bf16[3,2,128,6144]{3,2,1,0:T(8,128)(2,1)} %bitcast.124, bf16[1,256,6144]{2,1,0:T(8,128)(2,1)S(1)} %copy-done.1, f32[6144]{0:T(1024)S(1)} %bitcast.130, f32[256]{0:T(256)S(1)} %get-tuple-element.28, f32[256]{0:T(256)S(1)} %get-tuple-element.27), kind=kOutput, calls=%fused_computation.22 | convolution fusion | flops 2423783424 | bytes 13395968 | tf_op jit(solution)/shard_map/dot_general | solution.py:35
  96.9 0.7 copy-done.3
  97.6 1.2 fusion.27
  98.8 1.5 convolution_convert_fusion.3
  100.3 2.7 fusion.2
  103.0 4.7 %copy.34 = bf16[6144,256]{1,0:T(8,128)(2,1)} copy(bf16[6144,256]{0,1:T(8,128)(2,1)} %fusion.2) | data formatting | bytes 6291456
  107.8 75.6 %reduce-scatter.7.cloned.1.call-done = bf16[384,256]{1,0:T(8,128)(2,1)} async-done(((bf16[6144,256]{1,0:T(8,128)(2,1)}), bf16[384,256]{1,0:T(8,128)(2,1)}) %reduce-scatter.7.cloned.1.call-update) | async-done | bytes 196624
  183.4 1.1 copy.35
  184.7 8.7 %collective-permute-done = bf16[256,384]{1,0:T(8,128)(2,1)S(1)} collective-permute-done((bf16[256,384]{1,0:T(8,128)(2,1)S(1)}, bf16[256,384]{1,0:T(8,128)(2,1)S(1)}, u32[]{:S(2)}, u32[]{:S(2)}) %collective-permute-start) | collective-permute-done | bytes 196640 | tf_op jit(solution)/shard_map/ppermute | solution.py:12
  194.1 68.2 %all-gather.4.cloned.1.call-done = bf16[256,6144]{1,0:T(8,128)(2,1)} async-done(((bf16[256,384]{1,0:T(8,128)(2,1)}), bf16[256,6144]{1,0:T(8,128)(2,1)}) %all-gather.4.cloned.1.call-update) | async-done | bytes 3145744 | tf_op jit(solution)/shard_map/all_gather | solution.py:33
  262.3 3.2 convert_reduce_fusion
  265.5 6.5 %fusion.13 = f32[256,3,2,128]{0,3,2,1:T(8,128)S(1)} fusion(bf16[3,2,128,6144]{3,2,1,0:T(8,128)(2,1)} %bitcast.125, bf16[256,6144]{1,0:T(8,128)(2,1)} %all-gather.4.cloned.1.call-done, f32[256]{0:T(256)S(1)} %get-tuple-element.24, f32[256]{0:T(256)S(1)} %get-tuple-element.23, f32[6144]{0:T(1024)} %bitcast.129), kind=kOutput, calls=%fused_computation.20 | convolution fusion | flops 2423783424 | bytes 13395968 | tf_op jit(solution)/shard_map/dot_general | solution.py:35
  272.2 0.7 copy-done.2
  272.9 1.1 fusion.26
  274.0 1.6 convolution_convert_fusion.2
  275.6 2.7 fusion.3
  278.3 4.7 %copy.36 = bf16[6144,256]{1,0:T(8,128)(2,1)} copy(bf16[6144,256]{0,1:T(8,128)(2,1)} %fusion.3) | data formatting | bytes 6291456
  283.0 75.7 %reduce-scatter.9.cloned.1.call-done = bf16[384,256]{1,0:T(8,128)(2,1)} async-done(((bf16[6144,256]{1,0:T(8,128)(2,1)}), bf16[384,256]{1,0:T(8,128)(2,1)}) %reduce-scatter.9.cloned.1.call-update) | async-done | bytes 196624
  358.7 1.1 copy.37
  360.0 8.7 %collective-permute-done.1 = bf16[256,384]{1,0:T(8,128)(2,1)S(1)} collective-permute-done((bf16[256,384]{1,0:T(8,128)(2,1)S(1)}, bf16[256,384]{1,0:T(8,128)(2,1)S(1)}, u32[]{:S(2)}, u32[]{:S(2)}) %collective-permute-start.1) | collective-permute-done | bytes 196640 | tf_op jit(solution)/shard_map/ppermute | solution.py:12
  (39 shorter events, 2.8 us)
Async XLA Ops:
  6.5 93.8 %copy-start = (bf16[1,256,6144]{2,1,0:T(8,128)(2,1)S(1)}, bf16[1,256,6144]{2,1,0:T(8,128)(2,1)}, u32[]{:S(2)}) copy-start(bf16[1,256,6144]{2,1,0:T(8,128)(2,1)} %param.9) | copy-start | bytes 9437188
  6.5 79.1 %all-gather.6.cloned.1.call-start = ((), (), s32[]{:S(2)}) async-start(), calls=%async_computation.3 | async-start | bytes 3342336 | tf_op jit(solution)/shard_map/all_gather | solution.py:33
  7.3 12.9 %copy-start.7 = (f32[1,2,128]{2,1,0:T(2,128)S(1)}, f32[1,2,128]{2,1,0:T(2,128)}, u32[]{:S(2)}) copy-start(f32[1,2,128]{2,1,0:T(2,128)} %param.8) | copy-start | bytes 3076
  7.3 176.2 %reduce-scatter.7.cloned.1.call-start = ((), (), s32[]{:S(2)}) async-start(), calls=%async_computation.4 | async-start | bytes 3342336
  20.2 70.6 %copy-start.8 = (f32[1,6144]{1,0:T(1,128)S(1)}, f32[1,6144]{1,0:T(1,128)}, u32[]{:S(2)}) copy-start(f32[1,6144]{1,0:T(1,128)} %param.6) | copy-start | bytes 73732
  85.6 5.2 %copy-start.1 = (bf16[1,256,6144]{2,1,0:T(8,128)(2,1)S(1)}, bf16[1,256,6144]{2,1,0:T(8,128)(2,1)}, u32[]{:S(2)}) copy-start(bf16[1,256,6144]{2,1,0:T(8,128)(2,1)} %all-gather.6.cloned.1.call-done) | copy-start | bytes 9437188
  96.8 0.9 copy-start.3
  103.0 81.5 %copy-start.4 = (bf16[1,256,384]{2,1,0:T(8,128)(2,1)S(1)}, bf16[1,256,384]{2,1,0:T(8,128)(2,1)}, u32[]{:S(2)}) copy-start(bf16[1,256,384]{2,1,0:T(8,128)(2,1)} %param.5) | copy-start | bytes 589828
  107.7 154.6 %all-gather.4.cloned.1.call-start = ((), (), s32[]{:S(2)}) async-start(), calls=%async_computation.2 | async-start | bytes 3342336 | tf_op jit(solution)/shard_map/all_gather | solution.py:33
  184.6 8.8 %collective-permute-start = (bf16[256,384]{1,0:T(8,128)(2,1)S(1)}, bf16[256,384]{1,0:T(8,128)(2,1)S(1)}, u32[]{:S(2)}, u32[]{:S(2)}) collective-permute-start(bf16[256,384]{1,0:T(8,128)(2,1)S(1)} %fusion.28), channel_id=1, source_target_pairs={{0,16},{16,32},{32,48},{48,64},{64,80},{80,96},{96,112},{112,128},... | collective-permute-start | bytes 589832 | tf_op jit(solution)/shard_map/ppermute | solution.py:12
  193.4 0.7 copy-start.5
  194.1 164.6 %reduce-scatter.9.cloned.1.call-start = ((), (), s32[]{:S(2)}) async-start(), calls=%async_computation.5 | async-start | bytes 3342336
  272.0 0.9 copy-start.2
  278.3 81.5 %copy-start.6 = (bf16[256,384]{1,0:T(8,128)(2,1)S(1)}, bf16[256,384]{1,0:T(8,128)(2,1)}, u32[]{:S(2)}) copy-start(bf16[256,384]{1,0:T(8,128)(2,1)} %copy-done.5) | copy-start | bytes 589828
  359.9 8.8 %collective-permute-start.1 = (bf16[256,384]{1,0:T(8,128)(2,1)S(1)}, bf16[256,384]{1,0:T(8,128)(2,1)S(1)}, u32[]{:S(2)}, u32[]{:S(2)}) collective-permute-start(bf16[256,384]{1,0:T(8,128)(2,1)S(1)} %fusion.29), channel_id=1, source_target_pairs={{0,16},{16,32},{32,48},{48,64},{64,80},{80,96},{96,112},{112,128},... | collective-permute-start | bytes 589832 | tf_op jit(solution)/shard_map/ppermute | solution.py:12
Sparse Core Ops, SparseCore 0:
  9.2 76.4 all-gather.5
  107.8 75.5 reduce-scatter.6
  194.2 68.0 all-gather.3
  283.1 75.5 reduce-scatter.8
where the time goes:
time: 377 us; the launch traced here: 376 us
  waiting for transfers between devices  303 us (80%)
  local copies, waits for them, and re-layouts  27.3 us (7%)
  matrix products  23.2 us (6%)
  between operations  13.3 us (4%)
  other arithmetic  8.71 us (2%)
    unnamed x6, waiting for transfers between devices  152 us
    all_gather x2, waiting for transfers between devices, on_device(): gathered = lax.all_gather(current, 'tensor', axis=1, tiled=True)  134 us
    unnamed x24, local copies, waits for them, and re-layouts  27.3 us
    ppermute x2, waiting for transfers between devices, passed_along(): lax.ppermute(shard, axis, [(i, (i + by) % peers) for i in range(peers)])  17.4 us
    dot_general x2, matrix products, on_device(): projected = jnp.dot(normed, qkv_flat, preferred_element_type=jnp.float32)  12.5 us
  transfers between devices with their start and end apart: 6, of which 6 were waited for; matrix products, arithmetic and copies ran while one was open for 3% of the time, Pallas kernels for 0%

commit v1 on v0

--- a/solution.py
+++ b/solution.py
@@ -30,7 +30,8 @@
     gain_row = ln_gain[0]
     norm_gains = qk_gain[0]
     for step_index in range(STEPS):
-        gathered = lax.all_gather(current, "tensor", axis=1, tiled=True)
+        sent = jnp.stack([current] * lax.axis_size("tensor"))
+        gathered = jnp.concatenate(lax.all_to_all(sent, "tensor", 0, 0), axis=1)
         normed = layer_norm(gathered.astype(jnp.float32), gain_row).astype(jnp.bfloat16)
         projected = jnp.dot(normed, qkv_flat, preferred_element_type=jnp.float32)
         projected = projected.reshape(patches, 3, local_heads, HD)

time: 377 us -> 395 us (1.048)
  waiting for transfers between devices: 303 us -> 230 us
  blocking collectives: 0 us -> 71.2 us
  local copies, waits for them, and re-layouts: 27.3 us -> 39.8 us
  starting transfers between devices: 0.29 us -> 9.71 us
    all_gather x2 -> x0, waiting for transfers between devices: 134 us -> none  [on_device(): gathered = lax.all_gather(current, 'tensor', axis=1, tiled=True)]
    all_to_all x0 -> x1, blocking collectives: none -> 71.2 us  [on_device(): gathered = jnp.concatenate(lax.all_to_all(sent, 'tensor', 0, 0), axis=1)]
    all_to_all x0 -> x1, waiting for transfers between devices: none -> 57.2 us  [on_device(): gathered = jnp.concatenate(lax.all_to_all(sent, 'tensor', 0, 0), axis=1)]
    all_to_all x0 -> x1, starting transfers between devices: none -> 9.46 us  [on_device(): gathered = jnp.concatenate(lax.all_to_all(sent, 'tensor', 0, 0), axis=1)]
    all_to_all x0 -> x2, local copies, waits for them, and re-layouts: none -> 9.39 us  [on_device(): gathered = jnp.concatenate(lax.all_to_all(sent, 'tensor', 0, 0), axis=1)]
    unnamed x6 -> x4, waiting for transfers between devices: 152 us -> 155 us
    unnamed x24 -> x27, local copies, waits for them, and re-layouts: 27.3 us -> 26.9 us
  transfers between devices with their start and end apart: 6 -> 5, of which waited for: 6 -> 5; matrix products, arithmetic and copies ran while one was open for 3% -> 4% of each run, Pallas kernels for 0% -> 0%
where the time goes in v1:
time: 395 us; the launch traced here: 394 us
  waiting for transfers between devices  230 us (58%)
  blocking collectives  71.2 us (18%)
  local copies, waits for them, and re-layouts  39.8 us (10%)
  matrix products  21.2 us (5%)
  between operations  13.6 us (3%)
  starting transfers between devices  9.71 us (2%)
  other arithmetic  9.15 us (2%)
    unnamed x4, waiting for transfers between devices  155 us
    all_to_all x1, blocking collectives, on_device(): gathered = jnp.concatenate(lax.all_to_all(sent, 'tensor', 0, 0), axis=1)  71.2 us
    all_to_all x1, waiting for transfers between devices, on_device(): gathered = jnp.concatenate(lax.all_to_all(sent, 'tensor', 0, 0), axis=1)  57.2 us
    unnamed x27, local copies, waits for them, and re-layouts  26.9 us
    ppermute x2, waiting for transfers between devices, passed_along(): lax.ppermute(shard, axis, [(i, (i + by) % peers) for i in range(peers)])  17.4 us
    dot_general x2, matrix products, on_device(): projected = jnp.dot(normed, qkv_flat, preferred_element_type=jnp.float32)  10.4 us
    all_to_all x1, starting transfers between devices, on_device(): gathered = jnp.concatenate(lax.all_to_all(sent, 'tensor', 0, 0), axis=1)  9.46 us
    all_to_all x2, local copies, waits for them, and re-layouts, on_device(): gathered = jnp.concatenate(lax.all_to_all(sent, 'tensor', 0, 0), axis=1)  9.39 us
  transfers between devices with their start and end apart: 5, of which 5 were waited for; matrix products, arithmetic and copies ran while one was open for 4% of the time, Pallas kernels for 0%

profile of v1, /device:TPU:16, one launch (start us, length us, event | category | flops | bytes accessed | tf_op | source)
XLA Modules:
  0.0 394.3 jit_solution(10069870483858540654)
XLA Ops:
  6.5 3.2 stack.4
  9.7 9.5 %all-to-all-start = ((bf16[16,256,384]{2,1,0:T(8,128)(2,1)}), bf16[16,256,384]{2,1,0:T(8,128)(2,1)}, u32[]{:S(2)}, u32[]{:S(2)}) async-start(bf16[16,256,384]{2,1,0:T(8,128)(2,1)} %stack.4), calls=%async_computation | async-start | bytes 6291456 | tf_op jit(solution)/shard_map/all_to_all | solution.py:34
  20.5 12.7 %copy.27 = bf16[1,6144,3,256]{1,3,2,0:T(8,128)(2,1)} copy(bf16[1,6144,3,256]{3,1,2,0:T(8,128)(2,1)} %param.7) | data formatting | bytes 18874368 | tf_op args[2]
  33.2 57.2 %all-to-all-done = bf16[16,256,384]{2,1,0:T(8,128)(2,1)} async-done(((bf16[16,256,384]{2,1,0:T(8,128)(2,1)}), bf16[16,256,384]{2,1,0:T(8,128)(2,1)}, u32[]{:S(2)}, u32[]{:S(2)}) %all-to-all-start) | async-done | bytes 3145760 | tf_op jit(solution)/shard_map/all_to_all | solution.py:34
  90.3 4.7 %copy.26 = bf16[16,256,384]{1,2,0:T(8,128)(2,1)} copy(bf16[16,256,384]{2,1,0:T(8,128)(2,1)} %all-to-all-done) | data formatting | bytes 6291456 | tf_op jit(solution)/shard_map/all_to_all | solution.py:34
  95.0 2.9 convert_reduce_fusion.1
  98.0 1.1 fusion.4
  99.1 5.2 %fusion.56 = f32[256,3,2,128]{0,3,2,1:T(8,128)S(1)} fusion(bf16[256,6144,1,1]{0,1,3,2:T(8,128)(2,1)S(1)} %bitcast.112, bf16[3,2,128,6144]{3,2,1,0:T(8,128)(2,1)} %bitcast.109), kind=kOutput, calls=%fused_computation.94 | convolution fusion | flops 2415919104 | bytes 13369344 | tf_op jit(solution)/shard_map/dot_general | solution.py:36
  105.2 1.2 fusion.13
  106.4 1.5 convolution_convert_fusion.3
  107.9 2.7 fusion
  110.6 4.6 %copy.47 = bf16[6144,256]{1,0:T(8,128)(2,1)} copy(bf16[6144,256]{0,1:T(8,128)(2,1)} %fusion) | data formatting | bytes 6291456
  115.3 79.5 %reduce-scatter.7.cloned.1.call-done = bf16[384,256]{1,0:T(8,128)(2,1)} async-done(((bf16[6144,256]{1,0:T(8,128)(2,1)}), bf16[384,256]{1,0:T(8,128)(2,1)}) %reduce-scatter.7.cloned.1.call-update) | async-done | bytes 196624
  196.1 8.7 %collective-permute-done = bf16[256,384]{1,0:T(8,128)(2,1)S(1)} collective-permute-done((bf16[256,384]{1,0:T(8,128)(2,1)S(1)}, bf16[256,384]{1,0:T(8,128)(2,1)S(1)}, u32[]{:S(2)}, u32[]{:S(2)}) %collective-permute-start) | collective-permute-done | bytes 196640 | tf_op jit(solution)/shard_map/ppermute | solution.py:12
  205.2 71.2 %all_to_all.10 = bf16[16,256,384]{2,1,0:T(8,128)(2,1)} all-to-all(bf16[16,256,384]{2,1,0:T(8,128)(2,1)S(1)} %stack.5), channel_id=1, replica_groups=mesh['section'=16,'tensor'=16] {'tensor'}, dimensions={0} | all-to-all | bytes 6291456 | tf_op jit(solution)/shard_map/all_to_all | solution.py:34
  276.4 4.7 %copy.32 = bf16[16,256,384]{1,2,0:T(8,128)(2,1)} copy(bf16[16,256,384]{2,1,0:T(8,128)(2,1)} %all_to_all.10) | data formatting | bytes 6291456 | tf_op jit(solution)/shard_map/all_to_all | solution.py:34
  281.1 2.9 convert_reduce_fusion
  284.0 1.1 fusion.8
  285.2 5.2 %fusion.57 = f32[256,3,2,128]{0,3,2,1:T(8,128)S(1)} fusion(bf16[256,6144,1,1]{0,1,3,2:T(8,128)(2,1)S(1)} %bitcast.111, bf16[3,2,128,6144]{3,2,1,0:T(8,128)(2,1)} %bitcast.110), kind=kOutput, calls=%fused_computation.95 | convolution fusion | flops 2415919104 | bytes 13369344 | tf_op jit(solution)/shard_map/dot_general | solution.py:36
  292.4 1.6 convolution_convert_fusion.2
  294.0 2.7 fusion.1
  296.7 4.6 %copy.49 = bf16[6144,256]{1,0:T(8,128)(2,1)} copy(bf16[6144,256]{0,1:T(8,128)(2,1)} %fusion.1) | data formatting | bytes 6291456
  301.4 75.5 %reduce-scatter.9.cloned.1.call-done = bf16[384,256]{1,0:T(8,128)(2,1)} async-done(((bf16[6144,256]{1,0:T(8,128)(2,1)}), bf16[384,256]{1,0:T(8,128)(2,1)}) %reduce-scatter.9.cloned.1.call-update) | async-done | bytes 196624
  378.1 8.7 %collective-permute-done.1 = bf16[256,384]{1,0:T(8,128)(2,1)S(1)} collective-permute-done((bf16[256,384]{1,0:T(8,128)(2,1)S(1)}, bf16[256,384]{1,0:T(8,128)(2,1)S(1)}, u32[]{:S(2)}, u32[]{:S(2)}) %collective-permute-start.1) | collective-permute-done | bytes 196640 | tf_op jit(solution)/shard_map/ppermute | solution.py:12
  (46 shorter events, 7.8 us)
Async XLA Ops:
  6.5 101.4 %copy-start = (bf16[1,256,6144]{2,1,0:T(8,128)(2,1)S(1)}, bf16[1,256,6144]{2,1,0:T(8,128)(2,1)}, u32[]{:S(2)}) copy-start(bf16[1,256,6144]{2,1,0:T(8,128)(2,1)} %param.9) | copy-start | bytes 9437188
  9.7 10.0 %copy-start.8 = (f32[1,6144]{1,0:T(1,128)S(1)}, f32[1,6144]{1,0:T(1,128)}, u32[]{:S(2)}) copy-start(f32[1,6144]{1,0:T(1,128)} %param.6) | copy-start | bytes 73732
  9.7 80.6 %all-to-all-start = ((bf16[16,256,384]{2,1,0:T(8,128)(2,1)}), bf16[16,256,384]{2,1,0:T(8,128)(2,1)}, u32[]{:S(2)}, u32[]{:S(2)}) async-start(bf16[16,256,384]{2,1,0:T(8,128)(2,1)} %stack.4), calls=%async_computation | async-start | bytes 6291456 | tf_op jit(solution)/shard_map/all_to_all | solution.py:34
  19.2 175.6 %reduce-scatter.7.cloned.1.call-start = ((), (), s32[]{:S(2)}) async-start(), calls=%async_computation.4 | async-start | bytes 3342336
  20.5 77.5 %copy-start.6 = (f32[16,384]{1,0:T(8,128)}, f32[16,384]{1,0:T(8,128)S(1)}, u32[]{:S(2)}) copy-start(f32[16,384]{1,0:T(8,128)S(1)} %mul.182) | copy-start | bytes 73732
  20.5 12.7 %copy-start.9 = (f32[1,2,128]{2,1,0:T(2,128)S(1)}, f32[1,2,128]{2,1,0:T(2,128)}, u32[]{:S(2)}) copy-start(f32[1,2,128]{2,1,0:T(2,128)} %param.8) | copy-start | bytes 3076
  95.0 2.9 copy-start.2
  104.3 0.9 copy-start.4
  115.3 80.7 %copy-start.5 = (bf16[1,256,384]{2,1,0:T(8,128)(2,1)S(1)}, bf16[1,256,384]{2,1,0:T(8,128)(2,1)}, u32[]{:S(2)}) copy-start(bf16[1,256,384]{2,1,0:T(8,128)(2,1)} %param.5) | copy-start | bytes 589828
  115.3 261.6 %reduce-scatter.9.cloned.1.call-start = ((), (), s32[]{:S(2)}) async-start(), calls=%async_computation.5 | async-start | bytes 3342336
  196.0 8.8 %collective-permute-start = (bf16[256,384]{1,0:T(8,128)(2,1)S(1)}, bf16[256,384]{1,0:T(8,128)(2,1)S(1)}, u32[]{:S(2)}, u32[]{:S(2)}) collective-permute-start(bf16[256,384]{1,0:T(8,128)(2,1)S(1)} %fusion.15), channel_id=1, source_target_pairs={{0,16},{16,32},{32,48},{48,64},{64,80},{80,96},{96,112},{112,128},... | collective-permute-start | bytes 589832 | tf_op jit(solution)/shard_map/ppermute | solution.py:12
  276.4 7.6 %copy-start.7 = (f32[16,384]{1,0:T(8,128)S(1)}, f32[16,384]{1,0:T(8,128)}, u32[]{:S(2)}) copy-start(f32[16,384]{1,0:T(8,128)} %copy-done.6) | copy-start | bytes 73732
  281.1 2.9 copy-start.1
  290.4 0.9 copy-start.3
  378.0 8.8 %collective-permute-start.1 = (bf16[256,384]{1,0:T(8,128)(2,1)S(1)}, bf16[256,384]{1,0:T(8,128)(2,1)S(1)}, u32[]{:S(2)}, u32[]{:S(2)}) collective-permute-start(bf16[256,384]{1,0:T(8,128)(2,1)S(1)} %fusion.14), channel_id=1, source_target_pairs={{0,16},{16,32},{32,48},{48,64},{64,80},{80,96},{96,112},{112,128},... | collective-permute-start | bytes 589832 | tf_op jit(solution)/shard_map/ppermute | solution.py:12
Sparse Core Ops, SparseCore 0:
  115.4 79.3 reduce-scatter.6
  301.5 75.3 reduce-scatter.8
